TPU v7x, 32 devices: a whole 2x2x4 slice. The times are simulated.
32 devices in a mesh: row: 4 (over x, core), col: 4 (over z), pt: 2 (over y).
Axes of the slice: x: 2, y: 2, z: 4, core: 2. Of those that a mesh axis runs over, the one named last changes fastest.
Arguments:
- first_factors: int32 [32, 1024, 1024], P('pt', 'row', 'col'), may hold values from 0 to 12288
- second_factors: int32 [32, 1024, 1024], P('pt', 'row', 'col'), may hold values from 0 to 12288
Outputs:
- scaled_product: float32 [45, 1024, 1024], P(None, ('row', 'pt'), 'col')
All inputs are finite; a program needn't handle non-finite values.
Results may differ from a plain program's by a relative error of at most 0.0003.
Values may be sent and summed in bfloat16 or wider, within the bound.
A program may use at most 128 MiB of HBM per device.

v0:
```python
import jax
import jax.numpy as jnp
import numpy as np
from jax import lax
from jax.sharding import PartitionSpec as P

DEG = 16
modulus = 12289
digit_base = 128


def primitive_root():
    for candidate in range(2, modulus):
        if pow(candidate, 6144, modulus) != 1 and pow(candidate, 4096, modulus) != 1:
            return candidate
    return 0


def make_table(order_size, row_count, column_count, inverse):
    generator = primitive_root()
    root_value = pow(generator, (modulus - 1) // order_size, modulus)
    scaling = 1
    if inverse:
        root_value = pow(root_value, modulus - 2, modulus)
        scaling = pow(order_size, modulus - 2, modulus)
    entries = [
        [
            pow(root_value, row_index * column_index % order_size, modulus) * scaling % modulus
            for column_index in range(column_count)
        ]
        for row_index in range(row_count)
    ]
    return np.array(entries, dtype=np.int64)


def value_digits(values):
    high_digit = values // digit_base
    return (
        high_digit.astype(jnp.bfloat16),
        (values - digit_base * high_digit).astype(jnp.bfloat16),
    )


def combine(high_high, high_low, low_high, low_low):
    top_part = high_high.astype(jnp.int32) % modulus
    middle_part = (high_low.astype(jnp.int32) + low_high.astype(jnp.int32)) % modulus
    return (
        top_part * (digit_base * digit_base) % modulus
        + middle_part * digit_base
        + low_low.astype(jnp.int32)
    ) % modulus


def transform(matrix_table, coefs):
    slot_count = coefs.shape[0]
    flat_coefs = coefs.reshape(slot_count, -1)
    table_high = jnp.asarray(matrix_table // digit_base, dtype=jnp.bfloat16)
    table_low = jnp.asarray(matrix_table % digit_base, dtype=jnp.bfloat16)
    data_high, data_low = value_digits(flat_coefs)

    def product_of(left_part, right_part):
        return jnp.dot(left_part, right_part, preferred_element_type=jnp.float32)

    mixed_values = combine(
        product_of(table_high, data_high),
        product_of(table_high, data_low),
        product_of(table_low, data_high),
        product_of(table_low, data_low),
    )
    return mixed_values.reshape(matrix_table.shape[0], coefs.shape[1], coefs.shape[2])


def batched_product(left_part, right_part):
    return jnp.einsum("bik,bkj->bij", left_part, right_part, preferred_element_type=jnp.float32)


def digit_sum(totals, left_digits, right_digits):
    return (
        totals[0] + batched_product(left_digits[0], right_digits[0]),
        totals[1] + batched_product(left_digits[0], right_digits[1]),
        totals[2] + batched_product(left_digits[1], right_digits[0]),
        totals[3] + batched_product(left_digits[1], right_digits[1]),
    )


def pointwise(left_values, right_values):
    left_points, right_points = (
        lax.all_to_all(
            lax.all_to_all(
                left_values.astype(jnp.float32), "col", split_axis=0, concat_axis=2, tiled=True
            ),
            "pt",
            split_axis=0,
            concat_axis=1,
            tiled=True,
        ),
        lax.all_to_all(
            lax.all_to_all(
                right_values.astype(jnp.float32), "col", split_axis=0, concat_axis=2, tiled=True
            ),
            "pt",
            split_axis=0,
            concat_axis=1,
            tiled=True,
        ),
    )
    left_digits = value_digits(left_points.astype(jnp.int32))
    right_digits = value_digits(right_points.astype(jnp.int32))
    zeros_init = jnp.zeros(left_points.shape, jnp.float32)
    column_parts = tuple((digit_part for digit_part in left_digits))
    totals = digit_sum(
        (zeros_init, zeros_init, zeros_init, zeros_init),
        column_parts,
        (
            lax.all_gather(right_digits[0], "row", axis=1, tiled=True),
            lax.all_gather(right_digits[1], "row", axis=1, tiled=True),
        ),
    )
    product_values = combine(totals[0], totals[1], totals[2], totals[3]).astype(jnp.float32)
    arrived = lax.all_to_all(
        lax.all_to_all(product_values, "col", split_axis=2, concat_axis=0, tiled=True),
        "pt",
        split_axis=1,
        concat_axis=0,
        tiled=True,
    )
    col_count = lax.axis_size("col")
    pt_count = lax.axis_size("pt")
    local_count = arrived.shape[0] // (col_count * pt_count)
    returned = arrived.reshape(pt_count, col_count, local_count, arrived.shape[1], arrived.shape[2])
    returned = returned.transpose(1, 0, 2, 3, 4).reshape(arrived.shape)
    return returned.astype(jnp.int32)


def local(first_factors, second_factors):
    forward_one = make_table(2 * DEG, 2 * DEG, DEG, False)
    inverse_one = make_table(2 * DEG, 2 * DEG, 2 * DEG, True)
    forward_two = make_table(4 * DEG, 4 * DEG, 2 * DEG, False)
    inverse_two = make_table(4 * DEG, 3 * DEG - 3, 4 * DEG, True)
    first_entries, second_entries = (
        lax.all_to_all(
            first_factors.astype(jnp.float32), "pt", split_axis=1, concat_axis=0, tiled=True
        ),
        lax.all_to_all(
            second_factors.astype(jnp.float32), "pt", split_axis=1, concat_axis=0, tiled=True
        ),
    )
    first_entries = first_entries.astype(jnp.int32)
    second_entries = second_entries.astype(jnp.int32)
    left_values = jnp.concatenate(
        [transform(forward_one, first_entries[:DEG]), transform(forward_one, first_entries[DEG:])],
        0,
    )
    right_values = jnp.concatenate(
        [
            transform(forward_one, second_entries[:DEG]),
            transform(forward_one, second_entries[DEG:]),
        ],
        0,
    )
    products = pointwise(left_values, right_values)
    first_product = transform(inverse_one, products[: 2 * DEG])
    second_product = transform(inverse_one, products[2 * DEG :])
    upper_values = transform(forward_two, first_product)
    lower_values = transform(forward_two[:, :DEG], second_product[DEG:])
    result_coefficients = transform(inverse_two, pointwise(upper_values, lower_values))
    return result_coefficients.astype(jnp.float32) / 12289.0


def reduce_centred(values):
    return values - 12289.0 * jnp.round(values * (1.0 / 12289.0))


def centred_digits(values):
    high_digit = jnp.round(values * (1.0 / 128.0))
    return (high_digit.astype(jnp.bfloat16), (values - 128.0 * high_digit).astype(jnp.bfloat16))


def combine_centred(high_high, middle, low_low):
    upper_part = reduce_centred(reduce_centred(high_high) * 128.0 + middle)
    return reduce_centred(upper_part * 128.0 + low_low)


def table_digits(matrix_table):
    centred = np.where(matrix_table > modulus // 2, matrix_table - modulus, matrix_table)
    high_digit = np.round(centred / 128.0)
    return (high_digit, centred - 128.0 * high_digit)


def centred_transform(table_high, table_low, coefs):
    data_high, data_low = centred_digits(coefs.astype(jnp.float32))
    table_high = jnp.asarray(table_high, dtype=jnp.bfloat16)
    table_low = jnp.asarray(table_low, dtype=jnp.bfloat16)

    def product_of(left_part, right_part):
        return jnp.einsum("ts,sab->tab", left_part, right_part, preferred_element_type=jnp.float32)

    middle = product_of(
        jnp.concatenate([table_high, table_low], 1), jnp.concatenate([data_low, data_high], 0)
    )
    return combine_centred(
        product_of(table_high, data_high), middle, product_of(table_low, data_low)
    )


def column_pointwise(left_values, right_values):
    right_points = lax.all_to_all(
        right_values.astype(jnp.int16), "col", split_axis=0, concat_axis=2, tiled=True
    )
    right_points = lax.all_gather(right_points, "row", axis=1, tiled=True)
    left_points = lax.all_to_all(
        left_values.astype(jnp.int16), "col", split_axis=0, concat_axis=2, tiled=True
    )
    left_high, left_low = centred_digits(left_points.astype(jnp.float32))
    right_high, right_low = centred_digits(right_points.astype(jnp.float32))
    middle = batched_product(left_high, right_low) + batched_product(left_low, right_high)
    product_values = combine_centred(
        batched_product(left_high, right_high), middle, batched_product(left_low, right_low)
    )
    return lax.all_to_all(
        product_values.astype(jnp.int16), "col", split_axis=2, concat_axis=0, tiled=True
    )


def pair_local(first_factors, second_factors):
    forward_one = table_digits(make_table(2 * DEG, 2 * DEG, DEG, False))
    inverse_one = table_digits(make_table(2 * DEG, 2 * DEG, 2 * DEG, True))
    forward_two = table_digits(make_table(4 * DEG, 4 * DEG, 2 * DEG, False))
    inverse_two = table_digits(make_table(4 * DEG, 3 * DEG - 3, 4 * DEG, True))
    half_points = 2 * DEG
    place = lax.axis_index("pt")
    products = column_pointwise(
        centred_transform(*forward_one, centre(first_factors)),
        centred_transform(*forward_one, centre(second_factors)),
    )
    own_product = centred_transform(*inverse_one, products).astype(jnp.int16)
    both_products = lax.all_gather(own_product, "pt", axis=0, tiled=True)
    first_product = both_products[: 2 * DEG]
    shifted = both_products[3 * DEG :]
    own_tables = [
        lax.dynamic_slice_in_dim(
            jnp.asarray(digit, dtype=jnp.bfloat16), place * half_points, half_points, 0
        )
        for digit in forward_two
    ]
    upper_values = centred_transform(*own_tables, first_product)
    lower_values = centred_transform(*[digit[:, :DEG] for digit in own_tables], shifted)
    products_two = column_pointwise(upper_values, lower_values)
    all_points = lax.all_to_all(products_two, "pt", split_axis=1, concat_axis=0, tiled=True)
    result = centred_transform(*inverse_two, all_points)
    return jnp.where(result < 0.0, result + 12289.0, result) / 12289.0


def centre(values):
    return jnp.where(values > modulus // 2, values - modulus, values)


def solution(mesh):
    in_specs = (P("pt", "row", "col"), P("pt", "row", "col"))
    out_specs = P(None, ("row", "pt"), "col")
    body = pair_local if mesh.shape["pt"] == 2 else local
    return jax.shard_map(body, mesh=mesh, in_specs=in_specs, out_specs=out_specs, check_vma=False)
```

profile of v0, /device:TPU:0, one launch (start us, length us, event | category | flops | bytes accessed | tf_op | source)
XLA Modules:
  0.0 1258.8 jit_solution(4259190581243966023)
XLA Ops:
  45.8 73.8 %all-to-all-done = s16[32,256,256]{2,1,0:T(8,128)(2,1)} async-done(((s16[32,256,256]{2,1,0:T(8,128)(2,1)}), s16[32,256,256]{2,1,0:T(8,128)(2,1)}, u32[]{:S(2)}, u32[]{:S(2)}) %all-to-all-start) | async-done | bytes 4194336 | tf_op jit(solution)/shard_map/all_to_all | solution.py:211
  131.8 12.0 copy.111
  143.8 10.8 reshape.16
  154.6 63.0 %all-to-all-done.1 = s16[32,256,256]{2,1,0:T(8,128)(2,1)} async-done(((s16[32,256,256]{2,1,0:T(8,128)(2,1)}), s16[32,256,256]{2,1,0:T(8,128)(2,1)}, u32[]{:S(2)}, u32[]{:S(2)}) %all-to-all-start.1) | async-done | bytes 4194336 | tf_op jit(solution)/shard_map/all_to_all | solution.py:207
  232.9 105.4 %all-gather.3 = s16[8,1024,1024]{2,1,0:T(8,128)(2,1)} all-gather(s16[8,256,1024]{2,1,0:T(8,128)(2,1)} %all_to_all.71), channel_id=1, replica_groups=mesh['row'=4,'col'=4,'pt'=2] {'row'}, dimensions={1}, use_global_device_ids=true | all-gather | bytes 20971520 | tf_op jit(solution)/shard_map/all_gather | solution.py:210
  338.4 16.5 %fusion.14 = f32[8,256,1024]{2,1,0:T(8,128)} fusion(s16[8,1024,1024]{2,1,0:T(8,128)(2,1)} %all-gather.3, f32[8,256,1024]{2,1,0:T(8,128)} %reshape.16), kind=kOutput, calls=%fused_computation.16 | convolution fusion | flops 4334813184 | bytes 33554432 | tf_op jit(solution)/shard_map/bik,bkj->bij/dot_general | solution.py:74
  354.9 17.6 %fusion.12 = f32[8,256,1024]{2,1,0:T(8,128)} fusion(s16[8,1024,1024]{2,1,0:T(8,128)(2,1)} %all-gather.3, f32[8,256,1024]{2,1,0:T(8,128)} %reshape.16), kind=kOutput, calls=%fused_computation.15 | convolution fusion | flops 4339007488 | bytes 33554432 | tf_op jit(solution)/shard_map/bik,bkj->bij/dot_general | solution.py:74
  372.5 18.3 %fusion.20 = f32[8,256,1024]{2,1,0:T(8,128)} fusion(s16[8,1024,1024]{2,1,0:T(8,128)(2,1)} %all-gather.3, f32[8,256,1024]{2,1,0:T(8,128)} %reshape.16), kind=kOutput, calls=%fused_computation.23 | convolution fusion | flops 4355784704 | bytes 33554432 | tf_op jit(solution)/shard_map/bik,bkj->bij/dot_general | solution.py:74
  390.8 25.6 %subtract_convert_fusion.5 = s16[8,256,1024]{2,1,0:T(8,128)(2,1)} fusion(f32[8,256,1024]{2,1,0:T(8,128)} %fusion.20, f32[8,256,1024]{2,1,0:T(8,128)} %fusion.12, f32[8,256,1024]{2,1,0:T(8,128)} %fusion.14, s16[8,1024,1024]{2,1,0:T(8,128)(2,1)} %all-gather.3, f32[8,256,1024]{2,1,0:T(8,128)} %reshape.16), kind=kOutput, calls=%fused_computation.59 | convolution fusion | flops 4389339136 | bytes 54525952 | tf_op jit(solution)/shard_map/bik,bkj->bij/dot_general | solution.py:74
  428.8 94.0 %all-to-all-done.2 = s16[8,256,1024]{1,0,2:T(8,128)(2,1)} async-done(((s16[8,256,1024]{1,0,2:T(8,128)(2,1)}), s16[8,256,1024]{1,0,2:T(8,128)(2,1)}, u32[]{:S(2)}, u32[]{:S(2)}) %all-to-all-start.2) | async-done | bytes 4194336 | tf_op jit(solution)/shard_map/all_to_all | solution.py:220
  529.3 10.5 copy.77
  555.1 92.8 %all-gather.4 = s16[64,256,256]{2,0,1:T(8,128)(2,1)S(1)} all-gather(s16[32,256,256]{2,0,1:T(8,128)(2,1)} %subtract_convert_fusion.4), channel_id=1, replica_groups=mesh['row'=4,'col'=4,'pt'=2] {'pt'}, dimensions={0}, use_global_device_ids=true | all-gather | bytes 12582912 | tf_op jit(solution)/shard_map/all_gather | solution.py:237
  657.1 10.0 subtract_convert_fusion.3
  698.0 70.7 %all-to-all-done.3 = s16[32,256,256]{2,1,0:T(8,128)(2,1)} async-done(((s16[32,256,256]{2,1,0:T(8,128)(2,1)}), s16[32,256,256]{2,1,0:T(8,128)(2,1)}, u32[]{:S(2)}, u32[]{:S(2)}) %all-to-all-start.3) | async-done | bytes 4194336 | tf_op jit(solution)/shard_map/all_to_all | solution.py:211
  780.6 12.0 copy.110
  792.6 10.8 reshape.18
  803.4 63.1 %all-to-all-done.4 = s16[32,256,256]{2,1,0:T(8,128)(2,1)} async-done(((s16[32,256,256]{2,1,0:T(8,128)(2,1)}), s16[32,256,256]{2,1,0:T(8,128)(2,1)}, u32[]{:S(2)}, u32[]{:S(2)}) %all-to-all-start.4) | async-done | bytes 4194336 | tf_op jit(solution)/shard_map/all_to_all | solution.py:207
  881.9 104.5 %all-gather.5 = s16[8,1024,1024]{2,1,0:T(8,128)(2,1)} all-gather(s16[8,256,1024]{2,1,0:T(8,128)(2,1)} %all_to_all.77), channel_id=1, replica_groups=mesh['row'=4,'col'=4,'pt'=2] {'row'}, dimensions={1}, use_global_device_ids=true | all-gather | bytes 20971520 | tf_op jit(solution)/shard_map/all_gather | solution.py:210
  986.4 16.5 %fusion.10 = f32[8,256,1024]{2,1,0:T(8,128)} fusion(s16[8,1024,1024]{2,1,0:T(8,128)(2,1)} %all-gather.5, f32[8,256,1024]{2,1,0:T(8,128)} %reshape.18), kind=kOutput, calls=%fused_computation.14 | convolution fusion | flops 4334813184 | bytes 33554432 | tf_op jit(solution)/shard_map/bik,bkj->bij/dot_general | solution.py:74
  1002.9 17.6 %fusion.8 = f32[8,256,1024]{2,1,0:T(8,128)} fusion(s16[8,1024,1024]{2,1,0:T(8,128)(2,1)} %all-gather.5, f32[8,256,1024]{2,1,0:T(8,128)} %reshape.18), kind=kOutput, calls=%fused_computation.13 | convolution fusion | flops 4339007488 | bytes 33554432 | tf_op jit(solution)/shard_map/bik,bkj->bij/dot_general | solution.py:74
  1020.5 18.3 %fusion.16 = f32[8,256,1024]{2,1,0:T(8,128)} fusion(s16[8,1024,1024]{2,1,0:T(8,128)(2,1)} %all-gather.5, f32[8,256,1024]{2,1,0:T(8,128)} %reshape.18), kind=kOutput, calls=%fused_computation.21 | convolution fusion | flops 4355784704 | bytes 33554432 | tf_op jit(solution)/shard_map/bik,bkj->bij/dot_general | solution.py:74
  1038.7 25.6 %subtract_convert_fusion = s16[8,256,1024]{2,1,0:T(8,128)(2,1)} fusion(f32[8,256,1024]{2,1,0:T(8,128)} %fusion.16, f32[8,256,1024]{2,1,0:T(8,128)} %fusion.8, f32[8,256,1024]{2,1,0:T(8,128)} %fusion.10, s16[8,1024,1024]{2,1,0:T(8,128)(2,1)} %all-gather.5, f32[8,256,1024]{2,1,0:T(8,128)} %reshape.18), kind=kOutput, calls=%fused_computation.52 | convolution fusion | flops 4389339136 | bytes 54525952 | tf_op jit(solution)/shard_map/bik,bkj->bij/dot_general | solution.py:74
  1071.5 99.7 %all_to_all.90 = s16[8,256,1024]{1,0,2:T(8,128)(2,1)} all-to-all(s16[8,256,1024]{1,0,2:T(8,128)(2,1)} %copy.84), channel_id=1, replica_groups=mesh['row'=4,'col'=4,'pt'=2] {'col'}, dimensions={2} | all-to-all | bytes 8388608 | tf_op jit(solution)/shard_map/all_to_all | solution.py:220
  1183.6 50.0 %all_to_all.91 = s16[32,256,256]{2,0,1:T(8,128)(2,1)S(1)} all-to-all(s16[32,256,256]{2,0,1:T(8,128)(2,1)S(1)} %copy.87), channel_id=1, replica_groups=mesh['row'=4,'col'=4,'pt'=2] {'pt'}, dimensions={1} | all-to-all | bytes 8388608 | tf_op jit(solution)/shard_map/all_to_all | solution.py:249
  (78 shorter events, 219.2 us)
Async XLA Ops:
  0.0 5.5 copy-start.3
  0.0 6.8 copy-start.2
  6.7 1.4 copy-start.11
  19.6 100.0 %all-to-all-start = ((s16[32,256,256]{2,1,0:T(8,128)(2,1)}), s16[32,256,256]{2,1,0:T(8,128)(2,1)}, u32[]{:S(2)}, u32[]{:S(2)}) async-start(s16[32,256,256]{2,1,0:T(8,128)(2,1)} %copy.69), calls=%async_computation | async-start | bytes 8388608 | tf_op jit(solution)/shard_map/all_to_all | solution.py:211
  119.6 98.0 %all-to-all-start.1 = ((s16[32,256,256]{2,1,0:T(8,128)(2,1)}), s16[32,256,256]{2,1,0:T(8,128)(2,1)}, u32[]{:S(2)}, u32[]{:S(2)}) async-start(s16[32,256,256]{2,1,0:T(8,128)(2,1)} %copy.74), calls=%async_computation.1 | async-start | bytes 8388608 | tf_op jit(solution)/shard_map/all_to_all | solution.py:207
  416.3 12.5 copy-start.1
  416.3 12.5 copy-start.4
  423.6 99.2 %all-to-all-start.2 = ((s16[8,256,1024]{1,0,2:T(8,128)(2,1)}), s16[8,256,1024]{1,0,2:T(8,128)(2,1)}, u32[]{:S(2)}, u32[]{:S(2)}) async-start(s16[8,256,1024]{1,0,2:T(8,128)(2,1)} %copy.76), calls=%async_computation.2 | async-start | bytes 8388608 | tf_op jit(solution)/shard_map/all_to_all | solution.py:220
  539.8 4.5 copy-start.8
  544.3 1.3 copy-start.7
  545.5 1.5 copy-start.10
  648.0 9.1 copy-start
  671.3 97.4 %all-to-all-start.3 = ((s16[32,256,256]{2,1,0:T(8,128)(2,1)}), s16[32,256,256]{2,1,0:T(8,128)(2,1)}, u32[]{:S(2)}, u32[]{:S(2)}) async-start(s16[32,256,256]{2,1,0:T(8,128)(2,1)} %copy.78), calls=%async_computation.3 | async-start | bytes 8388608 | tf_op jit(solution)/shard_map/all_to_all | solution.py:211
  676.4 4.3 slice-start
  679.4 2.2 slice-start.1
  768.7 97.8 %all-to-all-start.4 = ((s16[32,256,256]{2,1,0:T(8,128)(2,1)}), s16[32,256,256]{2,1,0:T(8,128)(2,1)}, u32[]{:S(2)}, u32[]{:S(2)}) async-start(s16[32,256,256]{2,1,0:T(8,128)(2,1)} %copy.82), calls=%async_computation.4 | async-start | bytes 8388608 | tf_op jit(solution)/shard_map/all_to_all | solution.py:207
  1242.3 2.2 copy-start.5
  1244.4 1.0 copy-start.6
  1245.4 1.5 copy-start.9
where the time goes:
time: 1270 us; the launch traced here: 1260 us
  blocking collectives  452 us (36%)
  waiting for transfers between devices  364 us (29%)
  matrix products  221 us (17%)
  local copies, waits for them, and re-layouts  148 us (12%)
  other arithmetic  45.2 us (4%)
  starting transfers between devices  27.2 us (2%)
    all_gather x2, blocking collectives, column_pointwise(): right_points = lax.all_gather(right_points, 'row', axis=1, tiled=True)  210 us
    dot_general x8, matrix products, batched_product(): jnp.einsum('bik,bkj->bij', left_part, right_part, preferred_element_type=...  156 us
    all_to_all x2, waiting for transfers between devices, column_pointwise(): lax.all_to_all(left_values.astype(jnp.int16), 'col', split_axis=0, concat...  144 us
    all_to_all x2, waiting for transfers between devices, column_pointwise(): lax.all_to_all(right_values.astype(jnp.int16), 'col', split_axis=0, conca...  126 us
    all_to_all x1, blocking collectives, column_pointwise(): lax.all_to_all(product_values.astype(jnp.int16), 'col', split_axis=2, con...  99.7 us
    all_to_all x1, waiting for transfers between devices, column_pointwise(): lax.all_to_all(product_values.astype(jnp.int16), 'col', split_axis=2, con...  94 us
    all_gather x1, blocking collectives, pair_local(): both_products = lax.all_gather(own_product, 'pt', axis=0, tiled=True)  92.8 us
    dot_general x18, matrix products, product_of(): jnp.einsum('ts,sab->tab', left_part, right_part, preferred_element_type=j...  65.3 us
  transfers between devices with their start and end apart: 5, of which 5 were waited for; matrix products, arithmetic and copies ran while one was open for 8% of the time, Pallas kernels for 0%

commit v1 on v0

--- a/solution.py
+++ b/solution.py
@@ -204,8 +204,15 @@
 
 
 def column_pointwise(left_values, right_values):
-    right_points = lax.all_to_all(
-        right_values.astype(jnp.int16), "col", split_axis=0, concat_axis=2, tiled=True
+    raw = right_values.astype(jnp.int16)
+    right_points = jnp.concatenate(
+        lax.all_to_all(
+            jnp.stack(jnp.split(raw, lax.axis_size("col"), axis=0)),
+            axis_name="col",
+            split_axis=0,
+            concat_axis=0,
+        ),
+        axis=2,
     )
     right_points = lax.all_gather(right_points, "row", axis=1, tiled=True)
     left_points = lax.all_to_all(

time: 1270 us -> 1200 us (0.945)
  waiting for transfers between devices: 364 us -> 303 us
    all_to_all x2, waiting for transfers between devices: 144 us -> 72.6 us  [column_pointwise(): lax.all_to_all(left_values.astype(jnp.int16), 'col', split_axis=0, concat...]
    all_to_all x4 -> x0, local copies, waits for them, and re-layouts: 30.7 us -> none  [column_pointwise(): lax.all_to_all(right_values.astype(jnp.int16), 'col', split_axis=0, conca...]
    reshape x0 -> x4, local copies, waits for them, and re-layouts: none -> 29.5 us  [column_pointwise(): jnp.concatenate(lax.all_to_all(jnp.stack(jnp.split(raw, lax.axis_size('co...]
  transfers between devices with their start and end apart: 5 -> 5, of which waited for: 5 -> 4; matrix products, arithmetic and copies ran while one was open for 8% -> 7% of each run, Pallas kernels for 0% -> 0%
where the time goes in v1:
time: 1200 us; the launch traced here: 1190 us
  blocking collectives  452 us (38%)
  waiting for transfers between devices  303 us (25%)
  matrix products  221 us (18%)
  local copies, waits for them, and re-layouts  138 us (12%)
  other arithmetic  49.2 us (4%)
  starting transfers between devices  27.4 us (2%)
    all_gather x2, blocking collectives, column_pointwise(): right_points = lax.all_gather(right_points, 'row', axis=1, tiled=True)  210 us
    dot_general x8, matrix products, batched_product(): jnp.einsum('bik,bkj->bij', left_part, right_part, preferred_element_type=...  156 us
    all_to_all x2, waiting for transfers between devices, column_pointwise(): lax.all_to_all(jnp.stack(jnp.split(raw, lax.axis_size('col'), axis=0)), a...  137 us
    all_to_all x1, blocking collectives, column_pointwise(): lax.all_to_all(product_values.astype(jnp.int16), 'col', split_axis=2, con...  99.6 us
    all_to_all x1, waiting for transfers between devices, column_pointwise(): lax.all_to_all(product_values.astype(jnp.int16), 'col', split_axis=2, con...  94 us
    all_gather x1, blocking collectives, pair_local(): both_products = lax.all_gather(own_product, 'pt', axis=0, tiled=True)  92.9 us
    all_to_all x2, waiting for transfers between devices, column_pointwise(): lax.all_to_all(left_values.astype(jnp.int16), 'col', split_axis=0, concat...  72.6 us
    dot_general x18, matrix products, product_of(): jnp.einsum('ts,sab->tab', left_part, right_part, preferred_element_type=j...  65.3 us
  transfers between devices with their start and end apart: 5, of which 4 were waited for; matrix products, arithmetic and copies ran while one was open for 7% of the time, Pallas kernels for 0%

profile of v1, /device:TPU:0, one launch (start us, length us, event | category | flops | bytes accessed | tf_op | source)
XLA Modules:
  0.0 1192.9 jit_solution(9691909683596180064)
XLA Ops:
  44.2 73.8 %all-to-all-done.1 = s16[4,8,256,256]{3,1,2,0:T(8,128)(2,1)} async-done(((s16[4,8,256,256]{3,1,2,0:T(8,128)(2,1)}), s16[4,8,256,256]{3,1,2,0:T(8,128)(2,1)}, u32[]{:S(2)}, u32[]{:S(2)}) %all-to-all-start.1) | async-done | bytes 4194336 | tf_op jit(solution)/shard_map/all_to_all | solution.py:209
  137.7 105.3 %all-gather.3 = s16[8,1024,1024]{2,1,0:T(8,128)(2,1)} all-gather(s16[8,256,1024]{2,1,0:T(8,128)(2,1)} %copy.75), channel_id=1, replica_groups=mesh['row'=4,'col'=4,'pt'=2] {'row'}, dimensions={1}, use_global_device_ids=true | all-gather | bytes 20971520 | tf_op jit(solution)/shard_map/all_gather | solution.py:217
  249.8 12.0 %copy.109 = f32[4,8,256,256]{3,0,2,1:T(4,128)} copy(f32[4,8,256,256]{3,2,1,0:T(8,128)} %convert.12) | data formatting | bytes 16777216 | tf_op jit(solution)/shard_map/convert_element_type | solution.py:221
  261.8 10.8 reshape.32
  272.6 16.7 %fusion.14 = f32[8,256,1024]{2,1,0:T(8,128)} fusion(s16[8,1024,1024]{2,1,0:T(8,128)(2,1)} %all-gather.3, f32[8,256,1024]{2,1,0:T(8,128)} %reshape.32), kind=kOutput, calls=%fused_computation.16 | convolution fusion | flops 4334813184 | bytes 33554432 | tf_op jit(solution)/shard_map/bik,bkj->bij/dot_general | solution.py:74
  289.3 17.6 %fusion.12 = f32[8,256,1024]{2,1,0:T(8,128)} fusion(s16[8,1024,1024]{2,1,0:T(8,128)(2,1)} %all-gather.3, f32[8,256,1024]{2,1,0:T(8,128)} %reshape.32), kind=kOutput, calls=%fused_computation.15 | convolution fusion | flops 4339007488 | bytes 33554432 | tf_op jit(solution)/shard_map/bik,bkj->bij/dot_general | solution.py:74
  306.9 18.3 %fusion.20 = f32[8,256,1024]{2,1,0:T(8,128)} fusion(s16[8,1024,1024]{2,1,0:T(8,128)(2,1)} %all-gather.3, f32[8,256,1024]{2,1,0:T(8,128)} %reshape.32), kind=kOutput, calls=%fused_computation.23 | convolution fusion | flops 4355784704 | bytes 33554432 | tf_op jit(solution)/shard_map/bik,bkj->bij/dot_general | solution.py:74
  325.2 25.6 %subtract_convert_fusion.5 = s16[8,256,1024]{2,1,0:T(8,128)(2,1)} fusion(f32[8,256,1024]{2,1,0:T(8,128)} %fusion.20, f32[8,256,1024]{2,1,0:T(8,128)} %fusion.12, f32[8,256,1024]{2,1,0:T(8,128)} %fusion.14, s16[8,1024,1024]{2,1,0:T(8,128)(2,1)} %all-gather.3, f32[8,256,1024]{2,1,0:T(8,128)} %reshape.32), kind=kOutput, calls=%fused_computation.59 | convolution fusion | flops 4389339136 | bytes 54525952 | tf_op jit(solution)/shard_map/bik,bkj->bij/dot_general | solution.py:74
  363.5 94.0 %all-to-all-done.2 = s16[8,256,1024]{1,0,2:T(8,128)(2,1)} async-done(((s16[8,256,1024]{1,0,2:T(8,128)(2,1)}), s16[8,256,1024]{1,0,2:T(8,128)(2,1)}, u32[]{:S(2)}, u32[]{:S(2)}) %all-to-all-start.2) | async-done | bytes 4194336 | tf_op jit(solution)/shard_map/all_to_all | solution.py:227
  464.0 10.5 copy.77
  489.8 92.9 %all-gather.4 = s16[64,256,256]{2,0,1:T(8,128)(2,1)S(1)} all-gather(s16[32,256,256]{2,0,1:T(8,128)(2,1)} %subtract_convert_fusion.4), channel_id=1, replica_groups=mesh['row'=4,'col'=4,'pt'=2] {'pt'}, dimensions={0}, use_global_device_ids=true | all-gather | bytes 12582912 | tf_op jit(solution)/shard_map/all_gather | solution.py:244
  591.5 10.0 subtract_convert_fusion.3
  617.4 8.5 subtract_convert_fusion.2
  630.6 72.6 %all-to-all-done.3 = s16[32,256,256]{2,1,0:T(8,128)(2,1)} async-done(((s16[32,256,256]{2,1,0:T(8,128)(2,1)}), s16[32,256,256]{2,1,0:T(8,128)(2,1)}, u32[]{:S(2)}, u32[]{:S(2)}) %all-to-all-start.3) | async-done | bytes 4194336 | tf_op jit(solution)/shard_map/all_to_all | solution.py:218
  715.2 12.0 %copy.108 = f32[4,8,256,256]{3,0,2,1:T(4,128)} copy(f32[4,8,256,256]{3,2,1,0:T(8,128)} %convert.14) | data formatting | bytes 16777216 | tf_op jit(solution)/shard_map/convert_element_type | solution.py:221
  727.2 10.8 reshape.34
  738.0 63.1 %all-to-all-done.4 = s16[4,8,256,256]{3,1,2,0:T(8,128)(2,1)} async-done(((s16[4,8,256,256]{3,1,2,0:T(8,128)(2,1)}), s16[4,8,256,256]{3,1,2,0:T(8,128)(2,1)}, u32[]{:S(2)}, u32[]{:S(2)}) %all-to-all-start.4) | async-done | bytes 4194336 | tf_op jit(solution)/shard_map/all_to_all | solution.py:209
  815.9 104.5 %all-gather.5 = s16[8,1024,1024]{2,1,0:T(8,128)(2,1)} all-gather(s16[8,256,1024]{2,1,0:T(8,128)(2,1)} %copy.83), channel_id=1, replica_groups=mesh['row'=4,'col'=4,'pt'=2] {'row'}, dimensions={1}, use_global_device_ids=true | all-gather | bytes 20971520 | tf_op jit(solution)/shard_map/all_gather | solution.py:217
  920.4 16.5 %fusion.10 = f32[8,256,1024]{2,1,0:T(8,128)} fusion(s16[8,1024,1024]{2,1,0:T(8,128)(2,1)} %all-gather.5, f32[8,256,1024]{2,1,0:T(8,128)} %reshape.34), kind=kOutput, calls=%fused_computation.14 | convolution fusion | flops 4334813184 | bytes 33554432 | tf_op jit(solution)/shard_map/bik,bkj->bij/dot_general | solution.py:74
  936.9 17.6 %fusion.8 = f32[8,256,1024]{2,1,0:T(8,128)} fusion(s16[8,1024,1024]{2,1,0:T(8,128)(2,1)} %all-gather.5, f32[8,256,1024]{2,1,0:T(8,128)} %reshape.34), kind=kOutput, calls=%fused_computation.13 | convolution fusion | flops 4339007488 | bytes 33554432 | tf_op jit(solution)/shard_map/bik,bkj->bij/dot_general | solution.py:74
  954.5 18.2 %fusion.16 = f32[8,256,1024]{2,1,0:T(8,128)} fusion(s16[8,1024,1024]{2,1,0:T(8,128)(2,1)} %all-gather.5, f32[8,256,1024]{2,1,0:T(8,128)} %reshape.34), kind=kOutput, calls=%fused_computation.21 | convolution fusion | flops 4355784704 | bytes 33554432 | tf_op jit(solution)/shard_map/bik,bkj->bij/dot_general | solution.py:74
  972.8 25.6 %subtract_convert_fusion = s16[8,256,1024]{2,1,0:T(8,128)(2,1)} fusion(f32[8,256,1024]{2,1,0:T(8,128)} %fusion.16, f32[8,256,1024]{2,1,0:T(8,128)} %fusion.8, f32[8,256,1024]{2,1,0:T(8,128)} %fusion.10, s16[8,1024,1024]{2,1,0:T(8,128)(2,1)} %all-gather.5, f32[8,256,1024]{2,1,0:T(8,128)} %reshape.34), kind=kOutput, calls=%fused_computation.52 | convolution fusion | flops 4389339136 | bytes 54525952 | tf_op jit(solution)/shard_map/bik,bkj->bij/dot_general | solution.py:74
  1005.6 99.6 %all_to_all.64 = s16[8,256,1024]{1,0,2:T(8,128)(2,1)} all-to-all(s16[8,256,1024]{1,0,2:T(8,128)(2,1)} %copy.84), channel_id=1, replica_groups=mesh['row'=4,'col'=4,'pt'=2] {'col'}, dimensions={2} | all-to-all | bytes 8388608 | tf_op jit(solution)/shard_map/all_to_all | solution.py:227
  1117.7 50.0 %all_to_all.65 = s16[32,256,256]{2,0,1:T(8,128)(2,1)S(1)} all-to-all(s16[32,256,256]{2,0,1:T(8,128)(2,1)S(1)} %copy.87), channel_id=1, replica_groups=mesh['row'=4,'col'=4,'pt'=2] {'pt'}, dimensions={1} | all-to-all | bytes 8388608 | tf_op jit(solution)/shard_map/all_to_all | solution.py:256
  (80 shorter events, 205.5 us)
Async XLA Ops:
  0.0 5.5 copy-start.3
  0.0 6.8 copy-start.2
  6.8 1.4 copy-start.11
  17.7 100.3 %all-to-all-start.1 = ((s16[4,8,256,256]{3,1,2,0:T(8,128)(2,1)}), s16[4,8,256,256]{3,1,2,0:T(8,128)(2,1)}, u32[]{:S(2)}, u32[]{:S(2)}) async-start(s16[4,8,256,256]{3,1,2,0:T(8,128)(2,1)} %pad_add_fusion), calls=%async_computation.1 | async-start | bytes 8388608 | tf_op jit(solution)/shard_map/all_to_all | solution.py:209
  118.0 124.9 %all-to-all-start = ((s16[32,256,256]{2,1,0:T(8,128)(2,1)}), s16[32,256,256]{2,1,0:T(8,128)(2,1)}, u32[]{:S(2)}, u32[]{:S(2)}) async-start(s16[32,256,256]{2,1,0:T(8,128)(2,1)} %copy.69), calls=%async_computation | async-start | bytes 8388608 | tf_op jit(solution)/shard_map/all_to_all | solution.py:218
  350.8 12.7 %copy-start.1 = (bf16[64,32]{1,0:T(8,128)(2,1)S(1)}, bf16[64,32]{1,0:T(8,128)(2,1)}, u32[]{:S(2)}) copy-start(bf16[64,32]{1,0:T(8,128)(2,1)} %constant.14.clone) | copy-start | bytes 12292
  350.8 12.7 %copy-start.4 = (bf16[64,32]{1,0:T(8,128)(2,1)S(1)}, bf16[64,32]{1,0:T(8,128)(2,1)}, u32[]{:S(2)}) copy-start(bf16[64,32]{1,0:T(8,128)(2,1)} %constant.13.clone) | copy-start | bytes 12292
  358.1 99.4 %all-to-all-start.2 = ((s16[8,256,1024]{1,0,2:T(8,128)(2,1)}), s16[8,256,1024]{1,0,2:T(8,128)(2,1)}, u32[]{:S(2)}, u32[]{:S(2)}) async-start(s16[8,256,1024]{1,0,2:T(8,128)(2,1)} %copy.76), calls=%async_computation.2 | async-start | bytes 8388608 | tf_op jit(solution)/shard_map/all_to_all | solution.py:227
  474.5 4.5 copy-start.8
  479.0 1.3 copy-start.7
  480.3 1.5 copy-start.10
  582.7 8.8 copy-start
  605.8 97.4 %all-to-all-start.3 = ((s16[32,256,256]{2,1,0:T(8,128)(2,1)}), s16[32,256,256]{2,1,0:T(8,128)(2,1)}, u32[]{:S(2)}, u32[]{:S(2)}) async-start(s16[32,256,256]{2,1,0:T(8,128)(2,1)} %copy.78), calls=%async_computation.3 | async-start | bytes 8388608 | tf_op jit(solution)/shard_map/all_to_all | solution.py:218
  610.9 4.3 slice-start
  613.9 2.2 slice-start.1
  703.2 97.9 %all-to-all-start.4 = ((s16[4,8,256,256]{3,1,2,0:T(8,128)(2,1)}), s16[4,8,256,256]{3,1,2,0:T(8,128)(2,1)}, u32[]{:S(2)}, u32[]{:S(2)}) async-start(s16[4,8,256,256]{3,1,2,0:T(8,128)(2,1)} %pad_add_fusion.1), calls=%async_computation.4 | async-start | bytes 8388608 | tf_op jit(solution)/shard_map/all_to_all | solution.py:209
  1176.3 2.2 copy-start.5
  1178.5 1.0 copy-start.6
  1179.5 1.5 copy-start.9
